TPU v7x, 32 devices: a whole 2x2x4 slice. The times are simulated.
32 devices in a mesh: groups: 2 (over y), space: 16 (over z, x, core).
Axes of the slice: x: 2, y: 2, z: 4, core: 2. Of those that a mesh axis runs over, the one named last changes fastest.
Arguments:
- modes: float32 [4, 128, 32, 64], P('groups', None, 'space'), parts along dimension 0, may hold values from -6 to 6
- cell_weight: float32 [32, 128], P('space', 'groups'), parts along dimension 1, may hold values from 0.5 to 2
- seeds: int32 [256], P(('groups', 'space')), parts along dimension 0, may hold values from 0 to 255
- coeff_table: float32 [256, 128], replicated, may hold values from -6 to 6
- force_table: float32 [256, 128], replicated, may hold values from -6 to 6
- visc_table: float32 [256], replicated, may hold values from 0.02 to 0.2
Outputs:
- coefficients: float32 [256, 128], P(('groups', 'space')), parts along dimension 0
There are 2 independent parts, one for each index of `groups`. A program takes and returns all parts, laid end to end along the dimension named above; an argument that names none is the same for every part. Nothing has to cross between parts.
All inputs are finite; a program needn't handle non-finite values.
Results may differ from a plain program's by a relative error of at most 0.00013.
Values sent between devices are 32-bit elements; how exact they have to be, the bound alone decides.
A program may use at most 64 MiB of HBM per device.

v0:
```python
import math

import jax
import jax.numpy as jnp
from jax import lax
from jax.sharding import PartitionSpec as P

STEPS = 2


TIME_STEP = 0.5


def padded_2(array, sides, width):
    for axis, dim in sides:
        devices, length = (lax.axis_size(axis), array.shape[dim])
        up = [(i, (i + 1) % devices) for i in range(devices)]
        down = [(j, i) for i, j in up]
        last = lax.slice_in_dim(array, length - width, length, axis=dim)
        first = lax.slice_in_dim(array, 0, width, axis=dim)
        before = lax.ppermute(last, axis, up)
        after = lax.ppermute(first, axis, down)
        array = jnp.concatenate([before, array, after], axis=dim)
    return array


def shards(modes, cell_weight, seeds, coeff_table, force_table, visc_table):
    mode_count = modes.shape[1]
    slab_cells = modes.shape[2]
    across = modes.shape[3]
    devices = lax.axis_size("space")
    cell_count = slab_cells * across
    total_cells = cell_count * devices
    padded = padded_2(modes, (("space", 2),), 2)
    slope_along = (
        padded[:, :, 0:slab_cells]
        - 8.0 * padded[:, :, 1 : slab_cells + 1]
        + 8.0 * padded[:, :, 3 : slab_cells + 3]
        - padded[:, :, 4 : slab_cells + 4]
    ) / 12.0
    slope_across = (
        jnp.roll(modes, 2, 3)
        - 8.0 * jnp.roll(modes, 1, 3)
        + 8.0 * jnp.roll(modes, -1, 3)
        - jnp.roll(modes, -2, 3)
    ) / 12.0
    slopes = jnp.stack([slope_along, slope_across]).reshape(2, 2, mode_count, cell_count)
    velocity = modes.reshape(2, mode_count, cell_count)
    cell_scale = cell_weight.reshape(cell_count) / total_cells
    weighted = velocity * cell_scale[None, None, :]
    diffusion = lax.psum(
        jnp.einsum(
            "taic,tajc->ij",
            slopes * cell_scale[None, None, None, :],
            slopes,
            precision=lax.Precision.HIGHEST,
        ),
        "space",
    )
    selector = (
        seeds[:, None] == jnp.arange(coeff_table.shape[0], dtype=jnp.int32)[None, :]
    ).astype(jnp.float32)
    coeffs = jnp.dot(selector, coeff_table, precision=lax.Precision.HIGHEST)
    forcing = jnp.dot(selector, force_table, precision=lax.Precision.HIGHEST)
    viscosity = jnp.dot(selector, visc_table, precision=lax.Precision.HIGHEST)
    own_count = coeffs.shape[0]

    def field_block(coeff_rows):
        flow = jnp.einsum("ni,aic->anc", coeff_rows, velocity, precision=lax.Precision.HIGHEST)
        grads = jnp.einsum("nk,takc->tanc", coeff_rows, slopes, precision=lax.Precision.HIGHEST)
        carried = jnp.sum(flow[:, None, :, :] * grads, axis=0)
        return jnp.einsum("aic,anc->ni", weighted, carried, precision=lax.Precision.HIGHEST)

    for repeat in range(STEPS):
        everyone = lax.all_gather(coeffs, "space", axis=0, tiled=True)
        rows_each = math.gcd(own_count * lax.axis_size("space"), 128)
        stacked = everyone.reshape(
            own_count * lax.axis_size("space") // rows_each, rows_each, mode_count
        )
        quadratic = lax.psum_scatter(
            lax.map(field_block, stacked).reshape(own_count * lax.axis_size("space"), mode_count),
            "space",
            scatter_dimension=0,
            tiled=True,
        )
        linear = jnp.dot(coeffs, diffusion, precision=lax.Precision.HIGHEST)
        coeffs = coeffs + TIME_STEP * (forcing - viscosity[:, None] * linear - quadratic)
    return coeffs


def solution(mesh):
    placed = (
        P("groups", None, "space", None),
        P("space", "groups"),
        P(("groups", "space")),
        P(),
        P(),
        P(),
    )
    return jax.shard_map(
        shards, mesh=mesh, in_specs=placed, out_specs=P(("groups", "space"), None), check_vma=False
    )
```

profile of v0, /device:TPU:0, one launch (start us, length us, event | category | flops | bytes accessed | tf_op | source)
XLA Modules:
  0.0 242.7 jit_solution(18027088971304564999)
XLA Ops:
  6.5 0.5 collective-permute-start
  7.0 5.0 %collective-permute-start.1 = (f32[2,128,2,64]{1,3,2,0:T(8,128)}, f32[2,128,2,64]{1,3,2,0:T(8,128)S(1)}, u32[]{:S(2)}, u32[]{:S(2)}) collective-permute-start(f32[2,128,2,64]{1,3,2,0:T(8,128)} %param.6), channel_id=1, source_target_pairs={{1,0},{2,1},{3,2},{4,3},{5,4},{6,5},{7,6},{8,7},{9,8},{10,9},{11,1... | collective-permute-start | bytes 393224 | tf_op jit(solution)/shard_map/ppermute | solution.py:22
  12.0 1.0 slice_bitcast_fusion
  13.1 0.1 fusion.23
  13.2 0.1 copy.35
  13.3 0.5 copy-done.4
  13.8 0.2 fusion.34
  14.0 19.5 %all_gather.6 = f32[128,128]{1,0:T(8,128)S(1)} all-gather(f32[8,128]{1,0:T(8,128)S(1)} %fusion.34), channel_id=1, replica_groups=mesh['groups'=2,'space'=16] {'space'}, dimensions={0}, use_global_device_ids=true | all-gather | bytes 69632 | tf_op jit(solution)/shard_map/all_gather | solution.py:75
  33.5 0.1 copy.39
  33.6 0.3 convolution_bitcast_fusion.3
  33.9 0.1 copy.37
  34.0 0.6 copy-done.5
  34.6 0.1 div.18
  34.7 0.7 copy-done.7
  35.3 0.6 dynamic-slice.2
  36.6 0.2 fusion.33
  36.8 0.1 copy.34
  36.9 0.6 fusion.2
  37.5 1.0 convolution_bitcast_fusion.6
  38.5 1.0 convolution_bitcast_fusion.5
  39.6 0.0 all-reduce.6.cloned.1.call-start
  39.6 0.6 copy-done.6
  40.3 0.2 convolution_bitcast_fusion.7
  40.5 85.0 %all-reduce.8.cloned.1.call-done = (f32[128,128]{1,0:T(8,128)}, f32[128,128]{1,0:T(8,128)}) async-done(((f32[128,128]{1,0:T(8,128)}, f32[128,128]{1,0:T(8,128)}), (f32[128,128]{1,0:T(8,128)}, f32[128,128]{1,0:T(8,128)})) %all-reduce.8.cloned.1.call-update) | async-done | bytes 131088 | tf_op jit(solution)/shard_map/psum | solution.py:51
  125.4 1.0 fusion.11
  126.4 22.2 %all_gather.7 = f32[128,128]{1,0:T(8,128)S(1)} all-gather(f32[8,128]{1,0:T(8,128)S(1)} %fusion.11), channel_id=1, replica_groups=mesh['groups'=2,'space'=16] {'space'}, dimensions={0}, use_global_device_ids=true | all-gather | bytes 69632 | tf_op jit(solution)/shard_map/all_gather | solution.py:75
  148.7 0.3 convolution_bitcast_fusion.2
  148.9 0.1 copy.42
  149.0 0.6 fusion.3
  149.7 1.0 convolution_bitcast_fusion.4
  150.7 83.7 %all-reduce.6.cloned.1.call-done = f32[128,128]{1,0:T(8,128)} async-done(((f32[128,128]{1,0:T(8,128)}), f32[128,128]{1,0:T(8,128)}) %all-reduce.6.cloned.1.call-update) | async-done | bytes 65552
  234.4 1.4 fusion.7
  (22 shorter events, 0.1 us)
Async XLA Ops:
  6.5 6.8 %copy-start = (f32[256,128]{1,0:T(8,128)S(1)}, f32[256,128]{1,0:T(8,128)}, u32[]{:S(2)}) copy-start(f32[256,128]{1,0:T(8,128)} %param.9) | copy-start | bytes 393220
  6.5 6.5 %copy-start.1 = (f32[2,128,2,64]{1,3,2,0:T(8,128)S(1)}, f32[2,128,2,64]{1,3,2,0:T(8,128)}, u32[]{:S(2)}) copy-start(f32[2,128,2,64]{1,3,2,0:T(8,128)} %param.6) | copy-start | bytes 393220
  6.5 118.9 %all-reduce.8.cloned.1.call-start = ((), (), s32[]{:S(2)}) async-start(), calls=%async_computation.1 | async-start | bytes 262144 | tf_op jit(solution)/shard_map/psum | solution.py:51
  6.5 30.2 %collective-permute-start = (f32[2,128,2,64]{1,3,2,0:T(8,128)}, f32[2,128,2,64]{1,3,2,0:T(8,128)S(1)}, u32[]{:S(2)}, u32[]{:S(2)}) collective-permute-start(f32[2,128,2,64]{1,3,2,0:T(8,128)} %param.6), channel_id=1, source_target_pairs={{0,1},{1,2},{2,3},{3,4},{4,5},{5,6},{6,7},{7,8},{8,9},{9,10},{10,1... | collective-permute-start | bytes 393224 | tf_op jit(solution)/shard_map/ppermute | solution.py:21
  7.0 29.8 %collective-permute-start.1 = (f32[2,128,2,64]{1,3,2,0:T(8,128)}, f32[2,128,2,64]{1,3,2,0:T(8,128)S(1)}, u32[]{:S(2)}, u32[]{:S(2)}) collective-permute-start(f32[2,128,2,64]{1,3,2,0:T(8,128)} %param.6), channel_id=1, source_target_pairs={{1,0},{2,1},{3,2},{4,3},{5,4},{6,5},{7,6},{8,7},{9,8},{10,9},{11,1... | collective-permute-start | bytes 393224 | tf_op jit(solution)/shard_map/ppermute | solution.py:22
  13.2 0.7 copy-start.4
  33.9 0.7 copy-start.5
  33.9 2.7 %copy-start.3 = (f32[256,128]{1,0:T(8,128)S(1)}, f32[256,128]{1,0:T(8,128)}, u32[]{:S(2)}) copy-start(f32[256,128]{1,0:T(8,128)} %param.10) | copy-start | bytes 393220
  34.7 0.7 copy-start.7
  39.6 0.7 copy-start.6
  39.6 194.8 %all-reduce.6.cloned.1.call-start = ((), (), s32[]{:S(2)}) async-start(), calls=%async_computation | async-start | bytes 131072
  150.7 83.7 %copy-start.2 = (f32[128,128]{1,0:T(8,128)S(1)}, f32[128,128]{1,0:T(8,128)}, u32[]{:S(2)}) copy-start(f32[128,128]{1,0:T(8,128)} %get-tuple-element.27) | copy-start | bytes 196612
Sparse Core Ops, SparseCore 0:
  39.7 85.6 all-reduce.7
  150.8 83.5 all-reduce.5
where the time goes:
time: 244 us; the launch traced here: 243 us
  waiting for transfers between devices  169 us (69%)
  blocking collectives  41.7 us (17%)
  between operations  14.2 us (6%)
  matrix products  7.8 us (3%)
  starting transfers between devices  5.55 us (2%)
  local copies, waits for them, and re-layouts  4.56 us (2%)
    psum x1, waiting for transfers between devices, shards(): lax.psum(jnp.einsum('taic,tajc->ij', slopes * cell_scale[None, None, None...  85 us
    unnamed x3, waiting for transfers between devices  83.7 us
    all_gather x2, blocking collectives, shards(): everyone = lax.all_gather(coeffs, 'space', axis=0, tiled=True)  41.7 us
    ppermute x1, starting transfers between devices, padded_2(): after = lax.ppermute(first, axis, down)  5.01 us
  transfers between devices with their start and end apart: 4, of which 2 were waited for; matrix products, arithmetic and copies ran while one was open for 1% of the time, Pallas kernels for 0%

commit v1 on v0

v1 whole, which is shorter than its diff:
```python
import functools

import jax
import jax.numpy as jnp
from jax import lax
from jax.experimental import pallas as pl
from jax.experimental.pallas import tpu as pltpu
from jax.sharding import PartitionSpec as P

STEPS = 2


TIME_STEP = 0.5

WIDTH = 2

HIGHEST = lax.Precision.HIGHEST

MESH = pl.DeviceIdType.MESH


def dot(a, b, contract=((1,), (0,))):
    return lax.dot_general(
        a, b, (contract, ((), ())), precision=HIGHEST, preferred_element_type=jnp.float32
    )


def kernel(
    n,
    across,
    modes_ref,
    weight_ref,
    seeds_ref,
    visc_ref,
    coeff_ref,
    force_ref,
    out_ref,
    halo,
    seeds_all,
    basis,
    fields,
    coeffs,
    partial,
    landed,
    halo_send,
    halo_recv,
    send_sem,
    recv_sem,
):
    me = lax.axis_index("space")
    own = seeds_ref.shape[0]
    modes_n = modes_ref.shape[1]
    cells = modes_ref.shape[2]
    edge = WIDTH * across
    params = coeff_ref.shape[0]
    total = own * n
    own_rows = pl.ds(pl.multiple_of(me * own, own), own)

    barrier = pltpu.get_barrier_semaphore()

    @pl.loop(1, n)
    def _(d):
        pl.semaphore_signal(
            barrier, inc=1, device_id={"space": lax.rem(me + d, n)}, device_id_type=MESH
        )

    def lateral(x, shift):
        lane = lax.rem(lax.broadcasted_iota(jnp.int32, x.shape, 1), across)
        inside = pltpu.roll(x, shift % cells, 1)
        around = pltpu.roll(x, (shift + (-across if shift > 0 else across)) % cells, 1)
        crossed = lane < shift if shift > 0 else lane >= across + shift
        return jnp.where(crossed, around, inside)

    for a in range(2):
        f = modes_ref[a]
        basis[:, a * cells : (a + 1) * cells] = f
        q = 4 + a
        basis[:, q * cells : (q + 1) * cells] = (
            lateral(f, 2) - 8.0 * lateral(f, 1) + 8.0 * lateral(f, -1) - lateral(f, -2)
        ) / 12.0
    seeds_all[own_rows, :] = seeds_ref[...]

    def selector(seeds):
        return (
            seeds[:, 0:1]
            == lax.broadcasted_iota(jnp.int32, (seeds.shape[0], params), 1)
        ).astype(jnp.float32)

    mine = selector(seeds_ref[...])
    forcing = dot(mine, force_ref[...])
    own_coeffs = dot(mine, coeff_ref[...])

    pl.semaphore_wait(barrier, n - 1)

    def halo_copy(src, slot, peer):
        return pltpu.make_async_remote_copy(
            src_ref=src,
            dst_ref=halo.at[slot],
            send_sem=halo_send.at[slot],
            recv_sem=halo_recv.at[slot],
            device_id={"space": peer},
            device_id_type=MESH,
        )

    def spread(phase, source, target):
        @pl.loop(1, n)
        def _(d):
            peer = lax.rem(me + d, n)
            pltpu.make_async_remote_copy(
                src_ref=source(peer),
                dst_ref=target(d),
                send_sem=send_sem.at[phase],
                recv_sem=recv_sem.at[phase],
                device_id={"space": peer},
                device_id_type=MESH,
            ).start()

    def whole(phase, ref):
        return pltpu.make_async_remote_copy(
            src_ref=ref,
            dst_ref=ref,
            send_sem=send_sem.at[phase],
            recv_sem=recv_sem.at[phase],
            device_id={"space": lax.rem(me + 1, n)},
            device_id_type=MESH,
        )

    up = halo_copy(modes_ref.at[:, :, pl.ds(cells - edge, edge)], 0, lax.rem(me + 1, n))
    down = halo_copy(modes_ref.at[:, :, pl.ds(0, edge)], 1, lax.rem(me + n - 1, n))
    spread(0, lambda peer: seeds_ref, lambda d: seeds_all.at[own_rows, :])
    up.start()
    down.start()

    seed_bytes = whole(0, seeds_all.at[pl.ds(0, total - own), :])
    seed_bytes.wait_recv()
    select = selector(seeds_all[...])
    now = dot(select, coeff_ref[...])
    viscosity = jnp.sum(select * visc_ref[...], axis=1, keepdims=True)
    up.wait_recv()
    down.wait_recv()
    for a in range(2):
        padded = jnp.concatenate([halo[0, a], modes_ref[a], halo[1, a]], axis=1)
        span = cells + 2 * edge
        slope = (
            pltpu.roll(padded, 2 * across, 1)
            - 8.0 * pltpu.roll(padded, across, 1)
            + 8.0 * pltpu.roll(padded, span - across, 1)
            - pltpu.roll(padded, span - 2 * across, 1)
        ) / 12.0
        q = 2 + a
        basis[:, q * cells : (q + 1) * cells] = slope[:, edge : edge + cells]

    scale = weight_ref[...] / (cells * n)
    for step in range(STEPS):
        gathered = dot(now, basis[...])
        part = [gathered[:, q * cells : (q + 1) * cells] for q in range(6)]
        for a in range(2):
            fields[:, a * cells : (a + 1) * cells] = scale * (
                part[0] * part[2 + a] + part[1] * part[4 + a]
            )
        damped = viscosity * scale
        for q in range(2, 6):
            fields[:, q * cells : (q + 1) * cells] = damped * part[q]
        partial[step] = dot(fields[...], basis[...], ((1,), (1,)))
        spread(
            1 + 2 * step,
            lambda peer: partial.at[step, pl.ds(pl.multiple_of(peer * own, own), own), :],
            lambda d: landed.at[step, d - 1],
        )
        change = partial[step, own_rows, :]
        whole(1 + 2 * step, landed.at[step]).wait_recv()
        change = change + jnp.sum(landed[step], axis=0)
        own_coeffs = own_coeffs + TIME_STEP * (forcing - change)
        if step < STEPS - 1:
            coeffs[step, own_rows, :] = own_coeffs
            spread(
                2 + 2 * step,
                lambda peer: coeffs.at[step, own_rows, :],
                lambda d: coeffs.at[step, own_rows, :],
            )
            whole(2 + 2 * step, coeffs.at[step, pl.ds(0, total - own), :]).wait_recv()
            now = coeffs[step]
    out_ref[...] = own_coeffs

    up.wait_send()
    down.wait_send()
    seed_bytes.wait_send()
    for step in range(STEPS):
        whole(1 + 2 * step, landed.at[step]).wait_send()
        if step < STEPS - 1:
            whole(2 + 2 * step, coeffs.at[step, pl.ds(0, total - own), :]).wait_send()


def shards(modes, cell_weight, seeds, coeff_table, force_table, visc_table):
    components, mode_count, slab_cells, across = modes.shape
    n = lax.axis_size("space")
    cells = slab_cells * across
    own = seeds.shape[0]
    total = own * n
    vmem = pl.BlockSpec(memory_space=pltpu.VMEM)
    return pl.pallas_call(
        functools.partial(kernel, n, across),
        out_shape=jax.ShapeDtypeStruct((own, mode_count), jnp.float32),
        in_specs=[vmem] * 6,
        out_specs=vmem,
        scratch_shapes=[
            pltpu.VMEM((2, components, mode_count, WIDTH * across), jnp.float32),
            pltpu.VMEM((total, 128), jnp.int32),
            pltpu.VMEM((mode_count, 6 * cells), jnp.float32),
            pltpu.VMEM((total, 6 * cells), jnp.float32),
            pltpu.VMEM((STEPS - 1, total, mode_count), jnp.float32),
            pltpu.VMEM((STEPS, total, mode_count), jnp.float32),
            pltpu.VMEM((STEPS, n - 1, own, mode_count), jnp.float32),
            pltpu.SemaphoreType.DMA((2,)),
            pltpu.SemaphoreType.DMA((2,)),
            pltpu.SemaphoreType.DMA((2 * STEPS,)),
            pltpu.SemaphoreType.DMA((2 * STEPS,)),
        ],
        compiler_params=pltpu.CompilerParams(collective_id=0, has_side_effects=True),
    )(
        modes.reshape(components, mode_count, cells),
        cell_weight.reshape(1, cells),
        jnp.broadcast_to(seeds[:, None], (own, 128)),
        visc_table.reshape(1, -1),
        coeff_table,
        force_table,
    )


def solution(mesh):
    placed = (
        P("groups", None, "space", None),
        P("space", "groups"),
        P(("groups", "space")),
        P(),
        P(),
        P(),
    )
    return jax.shard_map(
        shards, mesh=mesh, in_specs=placed, out_specs=P(("groups", "space"), None), check_vma=False
    )
```

time: 244 us -> 32.9 us (0.13)
  waiting for transfers between devices: 169 us -> 0 us
  blocking collectives: 41.7 us -> 0 us
  Pallas kernels: 0 us -> 27.8 us
  between operations: 14.2 us -> 0.01 us
  matrix products: 7.8 us -> 0 us
  starting transfers between devices: 5.55 us -> 0 us
    psum x1 -> x0, waiting for transfers between devices: 85 us -> none  [shards(): lax.psum(jnp.einsum('taic,tajc->ij', slopes * cell_scale[None, None, None...]
    unnamed x3 -> x0, waiting for transfers between devices: 83.7 us -> none
    all_gather x2 -> x0, blocking collectives: 41.7 us -> none  [shards(): everyone = lax.all_gather(coeffs, 'space', axis=0, tiled=True)]
    pallas_call x0 -> x1, Pallas kernels: none -> 27.8 us  [shards(): pl.pallas_call(functools.partial(kernel, n, across), out_shape=jax.ShapeD...]
    dot_general x12 -> x0, matrix products: 7.8 us -> none  [the longest x2 2.43 us: shards(): linear = jnp.dot(coeffs, diffusion, precision=lax.Precision.HIGHEST)]
    ppermute x2 -> x0, starting transfers between devices: 5.5 us -> none  [the longest x1 5.01 us: padded_2(): after = lax.ppermute(first, axis, down)]
  transfers between devices with their start and end apart: 4 -> 0, of which waited for: 2 -> 0; matrix products, arithmetic and copies ran while one was open for 1% -> 0% of each run, Pallas kernels for 0% -> 0%
where the time goes in v1:
time: 32.9 us; the launch traced here: 32.7 us
  Pallas kernels  27.8 us (84%)
  local copies, waits for them, and re-layouts  4.89 us (15%)
    pallas_call x1, Pallas kernels, shards(): pl.pallas_call(functools.partial(kernel, n, across), out_shape=jax.ShapeD...  27.8 us
    unnamed x5, local copies, waits for them, and re-layouts  1.98 us
    reshape x1, local copies, waits for them, and re-layouts, shards(): modes.reshape(components, mode_count, cells)  1.64 us
    broadcast_in_dim x1, local copies, waits for them, and re-layouts, shards(): jnp.broadcast_to(seeds[:, None], (own, 128))  0.66 us

profile of v1, /device:TPU:0, one launch (start us, length us, event | category | flops | bytes accessed | tf_op | source)
XLA Modules:
  0.0 32.7 jit_solution(14460593374363529052)
XLA Ops:
  0.0 0.0 copy-start.1
  0.0 0.7 %copy-done.1 = f32[2,64]{1,0:T(2,128)S(1)} copy-done((f32[2,64]{1,0:T(2,128)S(1)}, f32[2,64]{1,0:T(2,128)}, u32[]{:S(2)}) %copy-start.1) | copy-done | bytes 536
  0.7 0.0 copy-start
  0.7 0.6 %reshape.11.weight_ref = f32[1,128]{1,0:T(1,128)} reshape(f32[2,64]{1,0:T(2,128)S(1)} %copy-done.1) | data formatting | bytes 1024 | tf_op jit(solution)/shard_map/reshape | solution.py:222
  1.3 0.0 copy-done
  1.3 0.7 %broadcast_in_dim.2.seeds_ref = s32[8,128]{1,0:T(8,128)} broadcast(s32[8]{0:T(128)S(1)} %copy-done), dimensions={0} | broadcast | bytes 4128 | tf_op jit(solution)/shard_map/broadcast_in_dim | solution.py:223
  2.0 1.6 %copy.8.modes_ref = f32[2,128,128]{2,1,0:T(8,128)} copy(f32[2,128,128]{1,2,0:T(8,128)} %bitcast.2) | data formatting | bytes 262144 | tf_op jit(solution)/shard_map/reshape | solution.py:221
  3.6 27.8 %shard_map.64 = f32[8,128]{1,0:T(8,128)} custom-call(f32[2,128,128]{2,1,0:T(8,128)} %copy.8.modes_ref, f32[1,128]{1,0:T(1,128)} %reshape.11.weight_ref, s32[8,128]{1,0:T(8,128)} %broadcast_in_dim.2.seeds_ref, f32[1,256]{1,0:T(1,128)} %bitcast.3, f32[256,128]{1,0:T(8,128)} %coeff_ref.1, f32[256,128]{1,0:T(8,128)} %force_ref.1), custom_call_target="tpu_custom_call" | custom-call | tf_op jit(solution)/shard_map/pallas_call | solution.py:201
  31.5 1.3 %copy.10 = f32[8,128]{1,0:T(8,128)} copy(f32[8,128]{1,0:T(8,128)} %shard_map.64) | data formatting | bytes 8192
Async XLA Ops:
  0.0 0.7 %copy-start.1 = (f32[2,64]{1,0:T(2,128)S(1)}, f32[2,64]{1,0:T(2,128)}, u32[]{:S(2)}) copy-start(f32[2,64]{1,0:T(2,128)} %param.7) | copy-start | bytes 1540
  0.7 0.7 %copy-start = (s32[8]{0:T(128)S(1)}, s32[8]{0:T(128)}, u32[]{:S(2)}) copy-start(s32[8]{0:T(128)} %param.8) | copy-start | bytes 100

commit v2 on v1

v2 whole, which is shorter than its diff:
```python
import functools

import jax
import jax.numpy as jnp
from jax import lax
from jax.experimental import pallas as pl
from jax.experimental.pallas import tpu as pltpu
from jax.sharding import PartitionSpec as P

STEPS = 2


TIME_STEP = 0.5

MESH = pl.DeviceIdType.MESH

ROWS = ((1,), (0,))
LANES = ((1,), (1,))


def split(x):
    high = x.astype(jnp.bfloat16)
    return high, (x - high.astype(jnp.float32)).astype(jnp.bfloat16)


def product(a, b, contract):
    return lax.dot_general(a, b, (contract, ((), ())), preferred_element_type=jnp.float32)


def product_3(a, b, contract):
    return (
        product(a[0], b[1], contract) + product(a[1], b[0], contract)
    ) + product(a[0], b[0], contract)


def kernel(
    n,
    across,
    modes_hbm,
    weight_hbm,
    seeds_hbm,
    visc_hbm,
    coeff_hbm,
    force_hbm,
    out_ref,
    modes_ref,
    weight_ref,
    seeds_ref,
    visc_ref,
    coeff_ref,
    force_ref,
    seed_rows,
    high,
    low,
    coeffs,
    partial,
    landed,
    load_sem,
    halo_send,
    halo_recv,
    send_sem,
    recv_sem,
):
    me = lax.axis_index("space")
    own = seeds_hbm.shape[0]
    cells = modes_hbm.shape[1]
    slab = cells // across
    params = coeff_ref.shape[0]
    total = own * n
    own_rows = pl.ds(pl.multiple_of(me * own, own), own)
    before, after = lax.rem(me + n - 1, n), lax.rem(me + 1, n)

    barrier = pltpu.get_barrier_semaphore()

    @pl.loop(1, n)
    def _(d):
        pl.semaphore_signal(
            barrier, inc=1, device_id={"space": lax.rem(me + d, n)}, device_id_type=MESH
        )

    loads = [
        pltpu.make_async_copy(source, target, load_sem.at[i])
        for i, (source, target) in enumerate(
            (
                (seeds_hbm, seeds_ref),
                (modes_hbm, modes_ref.at[:, pl.ds(cells, cells), :]),
                (coeff_hbm, coeff_ref),
                (force_hbm, force_ref),
                (visc_hbm, visc_ref),
                (weight_hbm, weight_ref),
            )
        )
    ]
    for load in loads:
        load.start()
    loads[0].wait()
    lane = lax.broadcasted_iota(jnp.int32, (1, total), 1)
    row = jnp.zeros((1, total), jnp.int32)
    column = jnp.zeros((own, params), jnp.int32)
    for r in range(own):
        row = jnp.where(lane == me * own + r, seeds_ref[r], row)
        column = jnp.where(
            lax.broadcasted_iota(jnp.int32, (own, params), 0) == r, seeds_ref[r], column
        )
    seed_rows[0] = row
    loads[1].wait()

    pl.semaphore_wait(barrier, n - 1)

    def spread(phase, source, target):
        @pl.loop(1, n)
        def _(d):
            peer = lax.rem(me + d, n)
            pltpu.make_async_remote_copy(
                src_ref=source(peer),
                dst_ref=target(d),
                send_sem=send_sem.at[phase],
                recv_sem=recv_sem.at[phase],
                device_id={"space": peer},
                device_id_type=MESH,
            ).start()

    def whole(phase, ref):
        return pltpu.make_async_remote_copy(
            src_ref=ref,
            dst_ref=ref,
            send_sem=send_sem.at[phase],
            recv_sem=recv_sem.at[phase],
            device_id={"space": after},
            device_id_type=MESH,
        )

    def halo_copy(slot, place, peer):
        return pltpu.make_async_remote_copy(
            src_ref=modes_ref.at[:, pl.ds(cells, cells), :],
            dst_ref=modes_ref.at[:, pl.ds(place * cells, cells), :],
            send_sem=halo_send.at[slot],
            recv_sem=halo_recv.at[slot],
            device_id={"space": peer},
            device_id_type=MESH,
        )

    up = halo_copy(0, 0, after)
    down = halo_copy(1, 2, before)
    up.start()
    down.start()
    spread(0, lambda peer: seed_rows.at[0], lambda d: seed_rows.at[d])

    def keep(q, x):
        high[q * cells : (q + 1) * cells, :], low[q * cells : (q + 1) * cells, :] = split(x)

    def lateral(f, shift):
        layers = [
            pltpu.roll(f[s * across : (s + 1) * across], shift % across, 0) for s in range(slab)
        ]
        return jnp.concatenate(layers, axis=0)

    for a in range(2):
        f = modes_ref[a, cells : 2 * cells, :]
        keep(a, f)
        keep(
            4 + a,
            (lateral(f, 2) - 8.0 * lateral(f, 1) + 8.0 * lateral(f, -1) - lateral(f, -2)) / 12.0,
        )
    for load in loads[2:]:
        load.wait()
    mine = (column == lax.broadcasted_iota(jnp.int32, (own, params), 1)).astype(jnp.float32)
    forcing = lax.dot(mine, force_ref[...], precision=lax.Precision.HIGHEST)
    own_coeffs = lax.dot(mine, coeff_ref[...], precision=lax.Precision.HIGHEST)
    table = split(coeff_ref[...])
    scale = jnp.concatenate([weight_ref[s : s + 1, :] for s in range(slab)], axis=1) / (cells * n)

    seed_bytes = whole(0, seed_rows.at[pl.ds(1, n - 1)])
    seed_bytes.wait_recv()
    seeds = jnp.sum(seed_rows[...], axis=0)
    spot = jnp.broadcast_to(seeds.astype(jnp.float32), (128, total)).T
    spot = jnp.concatenate([spot] * (params // 128), axis=1)
    chosen = spot == lax.broadcasted_iota(jnp.int32, (total, params), 1).astype(jnp.float32)
    viscosity = jnp.sum(jnp.where(chosen, visc_ref[...], 0.0), axis=1, keepdims=True)
    chosen = chosen.astype(jnp.float32).astype(jnp.bfloat16)
    now = [product(chosen, half, ROWS).astype(jnp.bfloat16) for half in table]
    damped = viscosity * scale

    up.wait_recv()
    down.wait_recv()
    for a in range(2):
        f = [
            modes_ref[a, cells + shift * across : 2 * cells + shift * across, :]
            for shift in (-2, -1, 1, 2)
        ]
        keep(2 + a, (f[0] - 8.0 * f[1] + 8.0 * f[2] - f[3]) / 12.0)

    for step in range(STEPS):
        basis = (high[...], low[...])
        gathered = product_3(now, basis, LANES)
        part = [gathered[:, q * cells : (q + 1) * cells] for q in range(6)]
        fields = [scale * (part[0] * part[2 + a] + part[1] * part[4 + a]) for a in range(2)]
        fields += [damped * part[q] for q in range(2, 6)]
        partial[step] = product_3(split(jnp.concatenate(fields, axis=1)), basis, ROWS)
        spread(
            1 + 2 * step,
            lambda peer: partial.at[step, pl.ds(pl.multiple_of(peer * own, own), own), :],
            lambda d: landed.at[step, d - 1],
        )
        change = partial[step, own_rows, :]
        whole(1 + 2 * step, landed.at[step]).wait_recv()
        change = change + jnp.sum(landed[step], axis=0)
        own_coeffs = own_coeffs + TIME_STEP * (forcing - change)
        if step < STEPS - 1:
            coeffs[step, own_rows, :] = own_coeffs
            spread(
                2 + 2 * step,
                lambda peer: coeffs.at[step, own_rows, :],
                lambda d: coeffs.at[step, own_rows, :],
            )
            whole(2 + 2 * step, coeffs.at[step, pl.ds(0, total - own), :]).wait_recv()
            now = split(coeffs[step])
    out_ref[...] = own_coeffs

    up.wait_send()
    down.wait_send()
    seed_bytes.wait_send()
    for step in range(STEPS):
        whole(1 + 2 * step, landed.at[step]).wait_send()
        if step < STEPS - 1:
            whole(2 + 2 * step, coeffs.at[step, pl.ds(0, total - own), :]).wait_send()


def shards(modes, cell_weight, seeds, coeff_table, force_table, visc_table):
    components, mode_count, slab_cells, across = modes.shape
    n = lax.axis_size("space")
    cells = slab_cells * across
    own = seeds.shape[0]
    total = own * n
    params = coeff_table.shape[0]
    vmem = pl.BlockSpec(memory_space=pltpu.VMEM)
    return pl.pallas_call(
        functools.partial(kernel, n, across),
        out_shape=jax.ShapeDtypeStruct((own, mode_count), jnp.float32),
        in_specs=[pl.BlockSpec(memory_space=pl.ANY)] * 6,
        out_specs=vmem,
        scratch_shapes=[
            pltpu.VMEM((components, 3 * cells, mode_count), jnp.float32),
            pltpu.VMEM((slab_cells, across), jnp.float32),
            pltpu.SMEM((own,), jnp.int32),
            pltpu.VMEM((1, params), jnp.float32),
            pltpu.VMEM((params, mode_count), jnp.float32),
            pltpu.VMEM((params, mode_count), jnp.float32),
            pltpu.VMEM((n, 1, total), jnp.int32),
            pltpu.VMEM((6 * cells, mode_count), jnp.bfloat16),
            pltpu.VMEM((6 * cells, mode_count), jnp.bfloat16),
            pltpu.VMEM((STEPS - 1, total, mode_count), jnp.float32),
            pltpu.VMEM((STEPS, total, mode_count), jnp.float32),
            pltpu.VMEM((STEPS, n - 1, own, mode_count), jnp.float32),
            pltpu.SemaphoreType.DMA((6,)),
            pltpu.SemaphoreType.DMA((2,)),
            pltpu.SemaphoreType.DMA((2,)),
            pltpu.SemaphoreType.DMA((2 * STEPS,)),
            pltpu.SemaphoreType.DMA((2 * STEPS,)),
        ],
        compiler_params=pltpu.CompilerParams(collective_id=0, has_side_effects=True),
    )(
        modes.transpose(0, 2, 3, 1).reshape(components, cells, mode_count),
        cell_weight,
        seeds,
        visc_table.reshape(1, -1),
        coeff_table,
        force_table,
    )


def solution(mesh):
    placed = (
        P("groups", None, "space", None),
        P("space", "groups"),
        P(("groups", "space")),
        P(),
        P(),
        P(),
    )
    return jax.shard_map(
        shards, mesh=mesh, in_specs=placed, out_specs=P(("groups", "space"), None), check_vma=False
    )
```

time: 32.9 us -> 27.8 us (0.84)
  local copies, waits for them, and re-layouts: 4.89 us -> 1.28 us
  Pallas kernels: 27.8 us -> 26.3 us
    reshape x2 -> x0, local copies, waits for them, and re-layouts: 2.25 us -> none  [the longest x1 1.64 us: shards(): modes.reshape(components, mode_count, cells)]
    pallas_call x1, Pallas kernels: 27.8 us -> 26.3 us  [shards(): pl.pallas_call(functools.partial(kernel, n, across), out_shape=jax.ShapeD...]
    unnamed x5 -> x1, local copies, waits for them, and re-layouts: 1.98 us -> 1.28 us
    broadcast_in_dim x1 -> x0, local copies, waits for them, and re-layouts: 0.66 us -> none  [shards(): jnp.broadcast_to(seeds[:, None], (own, 128))]
where the time goes in v2:
time: 27.8 us; the launch traced here: 27.6 us
  Pallas kernels  26.3 us (95%)
  local copies, waits for them, and re-layouts  1.28 us (5%)
    pallas_call x1, Pallas kernels, shards(): pl.pallas_call(functools.partial(kernel, n, across), out_shape=jax.ShapeD...  26.3 us
    unnamed x1, local copies, waits for them, and re-layouts  1.28 us

profile of v2, /device:TPU:0, one launch (start us, length us, event | category | flops | bytes accessed | tf_op | source)
XLA Modules:
  0.0 27.6 jit_solution(3286631252082605349)
XLA Ops:
  0.0 26.3 %shard_map.64 = f32[8,128]{1,0:T(8,128)} custom-call(f32[2,128,128]{2,1,0:T(8,128)} %bitcast.4, f32[2,64]{1,0:T(2,128)} %weight_hbm.1, s32[8]{0:T(128)} %seeds_hbm.1, f32[1,256]{1,0:T(1,128)} %bitcast.5, f32[256,128]{1,0:T(8,128)} %coeff_hbm.1, f32[256,128]{1,0:T(8,128)} %force_hbm.1), custom_call_target="tpu_custom_call" | custom-call | tf_op jit(solution)/shard_map/pallas_call | solution.py:237
  26.3 1.3 %copy.8 = f32[8,128]{1,0:T(8,128)} copy(f32[8,128]{1,0:T(8,128)} %shard_map.64) | data formatting | bytes 8192

commit v3 on v2

v3 whole, which is shorter than its diff:
```python
import functools

import jax
import jax.numpy as jnp
from jax import lax
from jax.experimental import pallas as pl
from jax.experimental.pallas import tpu as pltpu
from jax.sharding import PartitionSpec as P

TIME_STEP = 0.5

MESH = pl.DeviceIdType.MESH

ROWS = ((1,), (0,))
LANES = ((1,), (1,))


def split(x):
    high = x.astype(jnp.bfloat16)
    return high, (x - high.astype(jnp.float32)).astype(jnp.bfloat16)


def product(a, b, contract):
    return lax.dot_general(a, b, (contract, ((), ())), preferred_element_type=jnp.float32)


BLOCK = 4


def product_3(a, b, contract):
    rows = a[0].shape[0]
    both = product(jnp.concatenate(a, axis=0), b[0], contract)
    return (product(a[0], b[1], contract) + both[rows:]) + both[:rows]


def kernel(
    n,
    across,
    modes_hbm,
    weight_hbm,
    seeds_hbm,
    visc_hbm,
    coeff_hbm,
    force_hbm,
    out_ref,
    slabs,
    weights,
    seeds_ref,
    visc_ref,
    coeff_ref,
    force_ref,
    seed_rows,
    spots,
    high,
    low,
    wide_high,
    wide_low,
    partial,
    landed,
    group_sum,
    group_landed,
    group_coeffs,
    group_force,
    last,
    last_landed,
    load_sem,
    slab_send,
    slab_recv,
    send_sem,
    recv_sem,
):
    me = lax.axis_index("space")
    blocks = n // BLOCK
    block, seat = me // BLOCK, lax.rem(me, BLOCK)
    base = me - seat
    own = seeds_hbm.shape[0]
    cells = modes_hbm.shape[1]
    mode_count = modes_hbm.shape[2]
    slab = cells // across
    params = coeff_ref.shape[0]
    total = own * n
    group = own * blocks
    partner = me + 1 - 2 * lax.rem(seat, 2)
    mirror = base + BLOCK - 1 - seat
    place = seat + 1
    high_end = seat // (BLOCK - 1)
    outer = high_end * (BLOCK + 1)
    beyond = lax.rem(me + n - 1 + 2 * high_end, n)
    at_end = (seat == 0) | (seat == BLOCK - 1)
    inside = jnp.logical_not(at_end)

    barrier = pltpu.get_barrier_semaphore()

    @pl.loop(1, n)
    def _(d):
        pl.semaphore_signal(
            barrier, inc=1, device_id={"space": lax.rem(me + d, n)}, device_id_type=MESH
        )

    loads = [
        pltpu.make_async_copy(source, target, load_sem.at[i])
        for i, (source, target) in enumerate(
            (
                (seeds_hbm, seeds_ref),
                (modes_hbm, slabs.at[:, place]),
                (weight_hbm, weights.at[seat]),
                (coeff_hbm, coeff_ref),
                (force_hbm, force_ref),
                (visc_hbm, visc_ref),
            )
        )
    ]
    for load in loads:
        load.start()
    loads[0].wait()
    lane = lax.broadcasted_iota(jnp.int32, (1, total), 1)
    row = jnp.zeros((1, total), jnp.int32)
    for r in range(own):
        row = jnp.where(lane == me * own + r, seeds_ref[r], row)
    seed_rows[0] = row
    loads[1].wait()
    loads[2].wait()

    pl.semaphore_wait(barrier, n - 1)

    def spread(phase, count, peer_of, source, target):
        @pl.loop(1, count)
        def _(d):
            peer = peer_of(d)
            pltpu.make_async_remote_copy(
                src_ref=source(peer),
                dst_ref=target(d),
                send_sem=send_sem.at[phase],
                recv_sem=recv_sem.at[phase],
                device_id={"space": peer},
                device_id_type=MESH,
            ).start()

    def anyone(d):
        return lax.rem(me + d, n)

    def in_block(d):
        return base + lax.rem(seat + d, BLOCK)

    def in_group(d):
        return lax.rem(me + BLOCK * d, n)

    def whole(phase, ref):
        return pltpu.make_async_remote_copy(
            src_ref=ref,
            dst_ref=ref,
            send_sem=send_sem.at[phase],
            recv_sem=recv_sem.at[phase],
            device_id={"space": partner},
            device_id_type=MESH,
        )

    def slab_copy(i, source, target, peer):
        return pltpu.make_async_remote_copy(
            src_ref=slabs.at[:, source],
            dst_ref=slabs.at[:, target],
            send_sem=slab_send.at[i],
            recv_sem=slab_recv.at[target],
            device_id={"space": peer},
            device_id_type=MESH,
        )

    def arrived(slot):
        slab_copy(0, slot, slot, partner).wait_recv()

    to_beyond = slab_copy(0, place, BLOCK + 1 - outer, beyond)
    to_mirror = slab_copy(1, place, place, mirror)
    to_partner = slab_copy(2, place, place, partner)

    @pl.when(at_end)
    def _():
        to_beyond.start()

    @pl.when(inside)
    def _():
        to_mirror.start()

    to_partner.start()
    spread(0, n, anyone, lambda peer: seed_rows.at[0], lambda d: seed_rows.at[d])
    spread(1, BLOCK, in_block, lambda peer: weights.at[seat], lambda d: weights.at[seat])

    def lateral(f, shift):
        layers = [
            pltpu.roll(f[s * across : (s + 1) * across], shift % across, 0)
            for s in range(f.shape[0] // across)
        ]
        return jnp.concatenate(layers, axis=0)

    def across_slope(f):
        return (
            lateral(f, 2) - 8.0 * lateral(f, 1) + 8.0 * lateral(f, -1) - lateral(f, -2)
        ) / 12.0

    def along_slope(f):
        width = f.shape[0] - 2 * cells
        g = [
            f[cells + shift * across : cells + width + shift * across] for shift in (-2, -1, 1, 2)
        ]
        return (g[0] - 8.0 * g[1] + 8.0 * g[2] - g[3]) / 12.0

    def keep(q, x):
        high[q * cells : (q + 1) * cells, :], low[q * cells : (q + 1) * cells, :] = split(x)

    for a in range(2):
        f = slabs[a, place]
        keep(a, f)
        keep(4 + a, across_slope(f))
    for load in loads[3:]:
        load.wait()
    table = split(coeff_ref[...])

    seed_bytes = whole(0, seed_rows.at[pl.ds(1, n - 1)])
    seed_bytes.wait_recv()
    seeds = jnp.sum(seed_rows[...], axis=0)
    spot = jnp.broadcast_to(seeds.astype(jnp.float32), (128, total)).T
    spots[...] = spot.reshape(blocks, BLOCK, own, 128)

    def choose(spot):
        spot = jnp.concatenate([spot] * (params // 128), axis=1)
        chosen = spot == lax.broadcasted_iota(jnp.int32, spot.shape, 1).astype(jnp.float32)
        viscosity = jnp.sum(jnp.where(chosen, visc_ref[...], 0.0), axis=1, keepdims=True)
        return chosen.astype(jnp.float32), viscosity

    chosen, viscosity = choose(spot)
    chosen = chosen.astype(jnp.bfloat16)
    now = [product(chosen, half, ROWS).astype(jnp.bfloat16) for half in table]

    def scale_of(held):
        parts = [w[s : s + 1, :] for w in held for s in range(slab)]
        return jnp.concatenate(parts, axis=1) / (cells * n)

    def advance(now, basis, scale, viscosity):
        gathered = product_3(now, basis, LANES)
        size = gathered.shape[1] // 6
        part = [gathered[:, q * size : (q + 1) * size] for q in range(6)]
        fields = [scale * (part[0] * part[2 + a] + part[1] * part[4 + a]) for a in range(2)]
        damped = viscosity * scale
        fields += [damped * part[q] for q in range(2, 6)]
        return product_3(split(jnp.concatenate(fields, axis=1)), basis, ROWS)

    arrived(seat)
    arrived(seat + 2)

    edge_partner = slab_copy(3, outer, outer, partner)
    edge_mirror = slab_copy(4, outer, outer, mirror)
    inner_partner = slab_copy(3, BLOCK - seat, BLOCK - seat, partner)

    @pl.when(at_end)
    def _():
        to_mirror.start()
        edge_partner.start()

    @pl.when(inside)
    def _():
        inner_partner.start()

    for a in range(2):
        f = slabs[a, pl.ds(seat, 3)].reshape(3 * cells, mode_count)
        keep(2 + a, along_slope(f))
    change = advance(now, (high[...], low[...]), scale_of([weights[seat]]), viscosity)
    partial[...] = change.reshape(blocks, BLOCK, own, mode_count)
    spread(
        2,
        BLOCK,
        in_block,
        lambda peer: partial.at[:, peer - base],
        lambda d: landed.at[d - 1],
    )

    @pl.when(at_end)
    def _():
        edge_mirror.start()

    chosen, viscosity = choose(spots[:, seat].reshape(group, 128))
    coeffs = lax.dot(chosen, coeff_ref[...], precision=lax.Precision.HIGHEST)
    forcing = lax.dot(chosen, force_ref[...], precision=lax.Precision.HIGHEST)
    weight_bytes = whole(1, weights.at[pl.ds(0, BLOCK - 1)])
    weight_bytes.wait_recv()
    scale = scale_of([weights[s] for s in range(BLOCK)])

    block_bytes = whole(2, landed)
    block_bytes.wait_recv()
    change = (partial[:, seat] + jnp.sum(landed[...], axis=0)).reshape(group, mode_count)
    group_sum[...] = change
    spread(3, blocks, in_group, lambda peer: group_sum, lambda d: group_landed.at[d - 1])

    other = BLOCK - seat
    late_1 = slab_copy(5, other, other, partner)
    late_2 = slab_copy(6, BLOCK + 1 - outer, BLOCK + 1 - outer, partner)

    @pl.when(at_end)
    def _():
        arrived(other)
        late_1.start()
        arrived(BLOCK + 1 - outer)
        late_2.start()
        arrived(3 - high_end)

    @pl.when(inside)
    def _():
        for k in range(3):
            arrived(lax.rem(seat + 3 + k, BLOCK + 2))

    size = BLOCK * cells

    def keep_wide(q, x):
        wide_high[q * size : (q + 1) * size, :], wide_low[q * size : (q + 1) * size, :] = split(x)

    for a in range(2):
        f = slabs[a].reshape((BLOCK + 2) * cells, mode_count)
        middle = f[cells : cells + size]
        keep_wide(a, middle)
        keep_wide(2 + a, along_slope(f))
        keep_wide(4 + a, across_slope(middle))

    group_bytes = whole(3, group_landed)
    group_bytes.wait_recv()
    change = change + jnp.sum(group_landed[...], axis=0)
    coeffs = coeffs + TIME_STEP * (forcing - change)
    group_coeffs[...] = coeffs.reshape(blocks, own, mode_count)
    group_force[...] = forcing.reshape(blocks, own, mode_count)
    change = advance(split(coeffs), (wide_high[...], wide_low[...]), scale, viscosity)
    last[...] = change.reshape(blocks, own, mode_count)
    spread(
        4, blocks, in_group, lambda peer: last.at[peer // BLOCK], lambda d: last_landed.at[d - 1]
    )
    last_bytes = whole(4, last_landed)
    last_bytes.wait_recv()
    change = last[block] + jnp.sum(last_landed[...], axis=0)
    out_ref[...] = group_coeffs[block] + TIME_STEP * (group_force[block] - change)

    to_mirror.wait_send()
    to_partner.wait_send()

    @pl.when(at_end)
    def _():
        for copy in (to_beyond, edge_partner, edge_mirror, late_1, late_2):
            copy.wait_send()

    @pl.when(inside)
    def _():
        inner_partner.wait_send()

    for sent in (seed_bytes, weight_bytes, block_bytes, group_bytes, last_bytes):
        sent.wait_send()


def shards(modes, cell_weight, seeds, coeff_table, force_table, visc_table):
    components, mode_count, slab_cells, across = modes.shape
    n = lax.axis_size("space")
    blocks = n // BLOCK
    cells = slab_cells * across
    own = seeds.shape[0]
    total = own * n
    params = coeff_table.shape[0]
    f32, bf16 = jnp.float32, jnp.bfloat16
    return pl.pallas_call(
        functools.partial(kernel, n, across),
        out_shape=jax.ShapeDtypeStruct((own, mode_count), f32),
        in_specs=[pl.BlockSpec(memory_space=pl.ANY)] * 6,
        out_specs=pl.BlockSpec(memory_space=pltpu.VMEM),
        scratch_shapes=[
            pltpu.VMEM((components, BLOCK + 2, cells, mode_count), f32),
            pltpu.VMEM((BLOCK, slab_cells, across), f32),
            pltpu.SMEM((own,), jnp.int32),
            pltpu.VMEM((1, params), f32),
            pltpu.VMEM((params, mode_count), f32),
            pltpu.VMEM((params, mode_count), f32),
            pltpu.VMEM((n, 1, total), jnp.int32),
            pltpu.VMEM((blocks, BLOCK, own, 128), f32),
            pltpu.VMEM((6 * cells, mode_count), bf16),
            pltpu.VMEM((6 * cells, mode_count), bf16),
            pltpu.VMEM((6 * BLOCK * cells, mode_count), bf16),
            pltpu.VMEM((6 * BLOCK * cells, mode_count), bf16),
            pltpu.VMEM((blocks, BLOCK, own, mode_count), f32),
            pltpu.VMEM((BLOCK - 1, blocks, own, mode_count), f32),
            pltpu.VMEM((own * blocks, mode_count), f32),
            pltpu.VMEM((blocks - 1, own * blocks, mode_count), f32),
            pltpu.VMEM((blocks, own, mode_count), f32),
            pltpu.VMEM((blocks, own, mode_count), f32),
            pltpu.VMEM((blocks, own, mode_count), f32),
            pltpu.VMEM((blocks - 1, own, mode_count), f32),
            pltpu.SemaphoreType.DMA((6,)),
            pltpu.SemaphoreType.DMA((7,)),
            pltpu.SemaphoreType.DMA((BLOCK + 2,)),
            pltpu.SemaphoreType.DMA((5,)),
            pltpu.SemaphoreType.DMA((5,)),
        ],
        compiler_params=pltpu.CompilerParams(collective_id=0, has_side_effects=True),
    )(
        modes.transpose(0, 2, 3, 1).reshape(components, cells, mode_count),
        cell_weight,
        seeds,
        visc_table.reshape(1, -1),
        coeff_table,
        force_table,
    )


def solution(mesh):
    placed = (
        P("groups", None, "space", None),
        P("space", "groups"),
        P(("groups", "space")),
        P(),
        P(),
        P(),
    )
    return jax.shard_map(
        shards, mesh=mesh, in_specs=placed, out_specs=P(("groups", "space"), None), check_vma=False
    )
```

time: 27.8 us -> 25.8 us (0.928)
  Pallas kernels: 26.3 us -> 24.4 us
    pallas_call x1, Pallas kernels: 26.3 us -> 24.4 us  [shards(): pl.pallas_call(functools.partial(kernel, n, across), out_shape=jax.ShapeD...]
where the time goes in v3:
time: 25.8 us; the launch traced here: 25.6 us
  Pallas kernels  24.4 us (95%)
  local copies, waits for them, and re-layouts  1.28 us (5%)
    pallas_call x1, Pallas kernels, shards(): pl.pallas_call(functools.partial(kernel, n, across), out_shape=jax.ShapeD...  24.4 us
    unnamed x1, local copies, waits for them, and re-layouts  1.28 us

profile of v3, /device:TPU:0, one launch (start us, length us, event | category | flops | bytes accessed | tf_op | source)
XLA Modules:
  0.0 25.6 jit_solution(10244727766370949892)
XLA Ops:
  0.0 24.4 %shard_map.64 = f32[8,128]{1,0:T(8,128)} custom-call(f32[2,128,128]{2,1,0:T(8,128)} %bitcast.4, f32[2,64]{1,0:T(2,128)} %weight_hbm.1, s32[8]{0:T(128)} %seeds_hbm.1, f32[1,256]{1,0:T(1,128)} %bitcast.5, f32[256,128]{1,0:T(8,128)} %coeff_hbm.1, f32[256,128]{1,0:T(8,128)} %force_hbm.1), custom_call_target="tpu_custom_call" | custom-call | tf_op jit(solution)/shard_map/pallas_call | solution.py:362
  24.4 1.3 %copy.8 = f32[8,128]{1,0:T(8,128)} copy(f32[8,128]{1,0:T(8,128)} %shard_map.64) | data formatting | bytes 8192

commit v4 on v3

--- a/solution.py
+++ b/solution.py
@@ -172,6 +172,8 @@
     to_mirror = slab_copy(1, place, place, mirror)
     to_partner = slab_copy(2, place, place, partner)
 
+    spread(0, n, anyone, lambda peer: seed_rows.at[0], lambda d: seed_rows.at[d])
+
     @pl.when(at_end)
     def _():
         to_beyond.start()
@@ -181,7 +183,6 @@
         to_mirror.start()
 
     to_partner.start()
-    spread(0, n, anyone, lambda peer: seed_rows.at[0], lambda d: seed_rows.at[d])
     spread(1, BLOCK, in_block, lambda peer: weights.at[seat], lambda d: weights.at[seat])
 
     def lateral(f, shift):
@@ -209,7 +210,7 @@
     for a in range(2):
         f = slabs[a, place]
         keep(a, f)
-        keep(4 + a, across_slope(f))
+        keep(2 + a, across_slope(f))
     for load in loads[3:]:
         load.wait()
     table = split(coeff_ref[...])
@@ -234,15 +235,19 @@
         parts = [w[s : s + 1, :] for w in held for s in range(slab)]
         return jnp.concatenate(parts, axis=1) / (cells * n)
 
-    def advance(now, basis, scale, viscosity):
-        gathered = product_3(now, basis, LANES)
-        size = gathered.shape[1] // 6
-        part = [gathered[:, q * size : (q + 1) * size] for q in range(6)]
-        fields = [scale * (part[0] * part[2 + a] + part[1] * part[4 + a]) for a in range(2)]
+    def pieces(now, high, low, start, count):
+        size = high.shape[0] // 6
+        rows = slice(start * size, (start + count) * size)
+        gathered = product_3(now, (high[rows, :], low[rows, :]), LANES)
+        return [gathered[:, q * size : (q + 1) * size] for q in range(count)]
+
+    def advance(part, basis, scale, viscosity):
+        fields = [scale * (part[0] * part[4 + a] + part[1] * part[2 + a]) for a in range(2)]
         damped = viscosity * scale
         fields += [damped * part[q] for q in range(2, 6)]
         return product_3(split(jnp.concatenate(fields, axis=1)), basis, ROWS)
 
+    part = pieces(now, high, low, 0, 4)
     arrived(seat)
     arrived(seat + 2)
 
@@ -261,8 +266,9 @@
 
     for a in range(2):
         f = slabs[a, pl.ds(seat, 3)].reshape(3 * cells, mode_count)
-        keep(2 + a, along_slope(f))
-    change = advance(now, (high[...], low[...]), scale_of([weights[seat]]), viscosity)
+        keep(4 + a, along_slope(f))
+    part += pieces(now, high, low, 4, 2)
+    change = advance(part, (high[...], low[...]), scale_of([weights[seat]]), viscosity)
     partial[...] = change.reshape(blocks, BLOCK, own, mode_count)
     spread(
         2,
@@ -315,8 +321,8 @@
         f = slabs[a].reshape((BLOCK + 2) * cells, mode_count)
         middle = f[cells : cells + size]
         keep_wide(a, middle)
-        keep_wide(2 + a, along_slope(f))
-        keep_wide(4 + a, across_slope(middle))
+        keep_wide(2 + a, across_slope(middle))
+        keep_wide(4 + a, along_slope(f))
 
     group_bytes = whole(3, group_landed)
     group_bytes.wait_recv()
@@ -324,7 +330,8 @@
     coeffs = coeffs + TIME_STEP * (forcing - change)
     group_coeffs[...] = coeffs.reshape(blocks, own, mode_count)
     group_force[...] = forcing.reshape(blocks, own, mode_count)
-    change = advance(split(coeffs), (wide_high[...], wide_low[...]), scale, viscosity)
+    part = pieces(split(coeffs), wide_high, wide_low, 0, 6)
+    change = advance(part, (wide_high[...], wide_low[...]), scale, viscosity)
     last[...] = change.reshape(blocks, own, mode_count)
     spread(
         4, blocks, in_group, lambda peer: last.at[peer // BLOCK], lambda d: last_landed.at[d - 1]
@@ -361,7 +368,7 @@
     f32, bf16 = jnp.float32, jnp.bfloat16
     return pl.pallas_call(
         functools.partial(kernel, n, across),
-        out_shape=jax.ShapeDtypeStruct((own, mode_count), f32),
+        out_shape=pltpu.VMEM((own, mode_count), f32),
         in_specs=[pl.BlockSpec(memory_space=pl.ANY)] * 6,
         out_specs=pl.BlockSpec(memory_space=pltpu.VMEM),
         scratch_shapes=[

time: 25.8 us -> 24.4 us (0.946)
  Pallas kernels: 24.4 us -> 23.6 us
  local copies, waits for them, and re-layouts: 1.28 us -> 0.6 us
    pallas_call x1, Pallas kernels: 24.4 us -> 23.6 us  [shards(): pl.pallas_call(functools.partial(kernel, n, across), out_shape=pltpu.VMEM...]
    unnamed x1, local copies, waits for them, and re-layouts: 1.28 us -> 0.6 us
where the time goes in v4:
time: 24.4 us; the launch traced here: 24.2 us
  Pallas kernels  23.6 us (97%)
  local copies, waits for them, and re-layouts  0.6 us (2%)
    pallas_call x1, Pallas kernels, shards(): pl.pallas_call(functools.partial(kernel, n, across), out_shape=pltpu.VMEM...  23.6 us
    unnamed x1, local copies, waits for them, and re-layouts  0.6 us

profile of v4, /device:TPU:0, one launch (start us, length us, event | category | flops | bytes accessed | tf_op | source)
XLA Modules:
  0.0 24.2 jit_solution(15111526041018118729)
XLA Ops:
  0.0 23.6 %shard_map.64 = f32[8,128]{1,0:T(8,128)S(1)} custom-call(f32[2,128,128]{2,1,0:T(8,128)} %bitcast.4, f32[2,64]{1,0:T(2,128)} %weight_hbm.1, s32[8]{0:T(128)} %seeds_hbm.1, f32[1,256]{1,0:T(1,128)} %bitcast.5, f32[256,128]{1,0:T(8,128)} %coeff_hbm.1, f32[256,128]{1,0:T(8,128)} %force_hbm.1), custom_call_target="tpu_custom_call" | custom-call | tf_op jit(solution)/shard_map/pallas_call | solution.py:369
  23.6 0.6 %copy.8 = f32[8,128]{1,0:T(8,128)} copy(f32[8,128]{1,0:T(8,128)S(1)} %shard_map.64) | data formatting | bytes 8192

commit v5 on v4

--- a/solution.py
+++ b/solution.py
@@ -25,6 +25,8 @@
 
 
 BLOCK = 4
+
+HALVES = 2
 
 
 def product_3(a, b, contract):
@@ -80,6 +82,7 @@
     params = coeff_ref.shape[0]
     total = own * n
     group = own * blocks
+    half = blocks // HALVES
     partner = me + 1 - 2 * lax.rem(seat, 2)
     mirror = base + BLOCK - 1 - seat
     place = seat + 1
@@ -268,15 +271,20 @@
         f = slabs[a, pl.ds(seat, 3)].reshape(3 * cells, mode_count)
         keep(4 + a, along_slope(f))
     part += pieces(now, high, low, 4, 2)
-    change = advance(part, (high[...], low[...]), scale_of([weights[seat]]), viscosity)
-    partial[...] = change.reshape(blocks, BLOCK, own, mode_count)
-    spread(
-        2,
-        BLOCK,
-        in_block,
-        lambda peer: partial.at[:, peer - base],
-        lambda d: landed.at[d - 1],
-    )
+    near_scale = scale_of([weights[seat]])
+    for h in range(HALVES):
+        rows = slice(h * total // HALVES, (h + 1) * total // HALVES)
+        change = advance(
+            [p[rows] for p in part], (high[...], low[...]), near_scale, viscosity[rows]
+        )
+        partial[h * half : (h + 1) * half] = change.reshape(half, BLOCK, own, mode_count)
+        spread(
+            2 + h,
+            BLOCK,
+            in_block,
+            lambda peer: partial.at[pl.ds(h * half, half), peer - base],
+            lambda d: landed.at[h, d - 1],
+        )
 
     @pl.when(at_end)
     def _():
@@ -289,11 +297,20 @@
     weight_bytes.wait_recv()
     scale = scale_of([weights[s] for s in range(BLOCK)])
 
-    block_bytes = whole(2, landed)
-    block_bytes.wait_recv()
-    change = (partial[:, seat] + jnp.sum(landed[...], axis=0)).reshape(group, mode_count)
-    group_sum[...] = change
-    spread(3, blocks, in_group, lambda peer: group_sum, lambda d: group_landed.at[d - 1])
+    sums, block_bytes, group_bytes = [], [], []
+    for h in range(HALVES):
+        block_bytes.append(whole(2 + h, landed.at[h]))
+        block_bytes[h].wait_recv()
+        summed = partial[h * half : (h + 1) * half, seat] + jnp.sum(landed[h], axis=0)
+        sums.append(summed.reshape(own * half, mode_count))
+        group_sum[h] = sums[h]
+        spread(
+            2 + HALVES + h,
+            blocks,
+            in_group,
+            lambda peer: group_sum.at[h],
+            lambda d: group_landed.at[h, d - 1],
+        )
 
     other = BLOCK - seat
     late_1 = slab_copy(5, other, other, partner)
@@ -324,9 +341,11 @@
         keep_wide(2 + a, across_slope(middle))
         keep_wide(4 + a, along_slope(f))
 
-    group_bytes = whole(3, group_landed)
-    group_bytes.wait_recv()
-    change = change + jnp.sum(group_landed[...], axis=0)
+    for h in range(HALVES):
+        group_bytes.append(whole(2 + HALVES + h, group_landed.at[h]))
+        group_bytes[h].wait_recv()
+        sums[h] = sums[h] + jnp.sum(group_landed[h], axis=0)
+    change = jnp.concatenate(sums, axis=0)
     coeffs = coeffs + TIME_STEP * (forcing - change)
     group_coeffs[...] = coeffs.reshape(blocks, own, mode_count)
     group_force[...] = forcing.reshape(blocks, own, mode_count)
@@ -334,9 +353,9 @@
     change = advance(part, (wide_high[...], wide_low[...]), scale, viscosity)
     last[...] = change.reshape(blocks, own, mode_count)
     spread(
-        4, blocks, in_group, lambda peer: last.at[peer // BLOCK], lambda d: last_landed.at[d - 1]
+        2 + 2 * HALVES, blocks, in_group, lambda peer: last.at[peer // BLOCK], lambda d: last_landed.at[d - 1]
     )
-    last_bytes = whole(4, last_landed)
+    last_bytes = whole(2 + 2 * HALVES, last_landed)
     last_bytes.wait_recv()
     change = last[block] + jnp.sum(last_landed[...], axis=0)
     out_ref[...] = group_coeffs[block] + TIME_STEP * (group_force[block] - change)
@@ -353,7 +372,7 @@
     def _():
         inner_partner.wait_send()
 
-    for sent in (seed_bytes, weight_bytes, block_bytes, group_bytes, last_bytes):
+    for sent in (seed_bytes, weight_bytes, *block_bytes, *group_bytes, last_bytes):
         sent.wait_send()
 
 
@@ -385,9 +404,9 @@
             pltpu.VMEM((6 * BLOCK * cells, mode_count), bf16),
             pltpu.VMEM((6 * BLOCK * cells, mode_count), bf16),
             pltpu.VMEM((blocks, BLOCK, own, mode_count), f32),
-            pltpu.VMEM((BLOCK - 1, blocks, own, mode_count), f32),
-            pltpu.VMEM((own * blocks, mode_count), f32),
-            pltpu.VMEM((blocks - 1, own * blocks, mode_count), f32),
+            pltpu.VMEM((HALVES, BLOCK - 1, blocks // HALVES, own, mode_count), f32),
+            pltpu.VMEM((HALVES, own * blocks // HALVES, mode_count), f32),
+            pltpu.VMEM((HALVES, blocks - 1, own * blocks // HALVES, mode_count), f32),
             pltpu.VMEM((blocks, own, mode_count), f32),
             pltpu.VMEM((blocks, own, mode_count), f32),
             pltpu.VMEM((blocks, own, mode_count), f32),
@@ -395,8 +414,8 @@
             pltpu.SemaphoreType.DMA((6,)),
             pltpu.SemaphoreType.DMA((7,)),
             pltpu.SemaphoreType.DMA((BLOCK + 2,)),
-            pltpu.SemaphoreType.DMA((5,)),
-            pltpu.SemaphoreType.DMA((5,)),
+            pltpu.SemaphoreType.DMA((3 + 2 * HALVES,)),
+            pltpu.SemaphoreType.DMA((3 + 2 * HALVES,)),
         ],
         compiler_params=pltpu.CompilerParams(collective_id=0, has_side_effects=True),
     )(

time: 24.4 us -> 24 us (0.984)
  Pallas kernels: 23.6 us -> 23.3 us
    pallas_call x1, Pallas kernels: 23.6 us -> 23.3 us  [shards(): pl.pallas_call(functools.partial(kernel, n, across), out_shape=pltpu.VMEM...]
where the time goes in v5:
time: 24 us; the launch traced here: 23.9 us
  Pallas kernels  23.3 us (97%)
  local copies, waits for them, and re-layouts  0.6 us (2%)
    pallas_call x1, Pallas kernels, shards(): pl.pallas_call(functools.partial(kernel, n, across), out_shape=pltpu.VMEM...  23.3 us
    unnamed x1, local copies, waits for them, and re-layouts  0.6 us

profile of v5, /device:TPU:0, one launch (start us, length us, event | category | flops | bytes accessed | tf_op | source)
XLA Modules:
  0.0 23.9 jit_solution(13287007917440684094)
XLA Ops:
  0.0 23.3 %shard_map.64 = f32[8,128]{1,0:T(8,128)S(1)} custom-call(f32[2,128,128]{2,1,0:T(8,128)} %bitcast.4, f32[2,64]{1,0:T(2,128)} %weight_hbm.1, s32[8]{0:T(128)} %seeds_hbm.1, f32[1,256]{1,0:T(1,128)} %bitcast.5, f32[256,128]{1,0:T(8,128)} %coeff_hbm.1, f32[256,128]{1,0:T(8,128)} %force_hbm.1), custom_call_target="tpu_custom_call" | custom-call | tf_op jit(solution)/shard_map/pallas_call | solution.py:388
  23.3 0.6 %copy.8 = f32[8,128]{1,0:T(8,128)} copy(f32[8,128]{1,0:T(8,128)S(1)} %shard_map.64) | data formatting | bytes 8192
